TPU v7x, 32 devices: a whole 2x2x4 slice. The times are simulated.
32 devices in a mesh: dp: 16 (over z, y, core), own: 2 (over x).
Axes of the slice: x: 2, y: 2, z: 4, core: 2. Of those that a mesh axis runs over, the one named last changes fastest.
Arguments:
- layer_inputs: bfloat16 [4, 16, 16, 128, 128], P(None, 'dp', 'own'), as said below
- weights: bfloat16 [4, 1152, 128], replicated, may hold values from -0.1875 to 0.1875
- top_cotangent: bfloat16 [16, 16, 128, 128], P('dp', 'own'), may hold values from -6 to 6
- segmentation: int32 [16, 16, 128], P('dp', 'own'), may hold values from 0 to 2
- layer_slots: int32 [4], replicated, may hold values from 0 to 3, as said below
- a_inverse: bfloat16 [4, 1152, 1152], P('own', 'dp'), as said below
- g_inverse: bfloat16 [4, 128, 128], P('own'), as said below
Outputs:
- preconditioned: float32 [4, 1152, 128], P(None, 'dp')
- input_grad: bfloat16 [16, 16, 128, 128], P('dp', 'own')
Inputs may be any that keep to these rules, and one draw needn't show every extreme that they name: Distinct slot numbers; layer l is held by owner layer_slots[l] // 2, in that owner's slot layer_slots[l] % 2. One owner holds exactly 2 layers in every draw. `a_inverse`: each factor is symmetric. `g_inverse`: each factor is symmetric. `layer_inputs`: activations after a rectifier.
All inputs are finite; a program needn't handle non-finite values.
Results may differ from a plain program's by a relative error of at most 0.011.
Values may be sent and summed in bfloat16 or wider, within the bound.
A program may use at most 64 MiB of HBM per device.

v0:
```python
import math
import jax
import jax.numpy as jnp
from jax import lax
from jax.sharding import PartitionSpec as P


def extended(cells, sides, width):
    for axis, dim in sides:
        count = lax.axis_size(axis)
        ends = count - 1
        head = lax.slice_in_dim(cells, 0, width, axis=dim)
        tail = lax.slice_in_dim(cells, cells.shape[dim] - width, cells.shape[dim], axis=dim)
        cells = jnp.concatenate(
            [
                lax.ppermute(tail, axis, [(i, (i + 1) % count) for i in range(ends)]),
                cells,
                lax.ppermute(head, axis, [((i + 1) % count, i) for i in range(ends)]),
            ],
            axis=dim,
        )
    return cells


def from_root(block, axis, owner):
    block = jnp.where(lax.axis_index(axis) == owner, block, jnp.zeros_like(block))
    return lax.psum(block, axis)


def loss_weight(labels):
    return jnp.where(labels == 0, 1.0, jnp.where(labels == 1, 0.0, 0.5)).astype(jnp.float32)


def tap_matrix(padded, num_rows, num_cols):
    channels = padded.shape[-1]
    pieces = []
    for tap_index in range(9):
        row_start = 2 - tap_index // 3
        col_start = 2 - tap_index % 3
        pieces.append(padded[row_start : row_start + num_rows, col_start : col_start + num_cols])
    stacked = jnp.stack(pieces, axis=2)
    return stacked.reshape(num_rows * num_cols, 9 * channels)


def per_device(
    layer_inputs, weights, top_cotangent, segmentation, layer_slots, a_inverse, g_inverse
):
    layer_count = layer_inputs.shape[0]
    num_rows = layer_inputs.shape[2]
    num_cols = layer_inputs.shape[3]
    channels = layer_inputs.shape[4]
    data_devices = lax.axis_size("dp")
    owner_devices = lax.axis_size("own")
    grad_scale = 1.0 / math.sqrt(data_devices * owner_devices * num_rows * num_cols)
    inputs_local = layer_inputs[:, 0]
    scaled = loss_weight(segmentation[0])[:, :, None] * top_cotangent[0].astype(jnp.float32)
    out_grad = scaled.astype(jnp.bfloat16)
    grad_blocks = [None] * layer_count
    input_grad = None
    for layer_index in range(layer_count - 1, -1, -1):
        rimmed = extended(out_grad, (("own", 0),), 1)
        padded = jnp.pad(rimmed, ((0, 0), (1, 1), (0, 0)))
        tap_rows = tap_matrix(padded, num_rows, num_cols)
        flat_inputs = inputs_local[layer_index].reshape(num_rows * num_cols, channels)
        grad_block = lax.dot_general(
            flat_inputs, tap_rows, (((0,), (0,)), ((), ())), preferred_element_type=jnp.float32
        )
        grad_blocks[layer_index] = grad_block.reshape(9 * channels, channels) * grad_scale
        kernel = weights[layer_index].reshape(channels, 9 * channels)
        input_side = lax.dot_general(
            tap_rows, kernel, (((1,), (1,)), ((), ())), preferred_element_type=jnp.float32
        )
        input_side = input_side.reshape(num_rows, num_cols, channels)
        if layer_index > 0:
            out_grad = jnp.where(inputs_local[layer_index] > 0, input_side, 0.0).astype(
                jnp.bfloat16
            )
        else:
            input_grad = input_side.astype(jnp.bfloat16)[None]
    grad_term = jnp.concatenate(grad_blocks, axis=1)
    grad_rows = lax.psum_scatter(grad_term, "dp", scatter_dimension=0, tiled=True)
    slot_count = a_inverse.shape[0]
    grad_sum = lax.psum(grad_rows.astype(jnp.bfloat16), "own")
    left_panels = []
    right_panels = []
    for layer_index in range(layer_count):
        slot_id = layer_slots[layer_index]
        owner_index = slot_id // slot_count
        local_slot = slot_id % slot_count
        left_panel = lax.dynamic_index_in_dim(a_inverse, local_slot, 0, keepdims=False)
        right_panel = lax.dynamic_index_in_dim(g_inverse, local_slot, 0, keepdims=False)
        left_panel, right_panel = (
            from_root(left_panel, "own", owner_index),
            from_root(right_panel, "own", owner_index),
        )
        left_panels.append(left_panel)
        right_panels.append(right_panel)
    left_stack = jnp.stack(left_panels, axis=0)
    right_stack = jnp.stack(right_panels, axis=0)
    gathered_piece = lax.all_gather(grad_sum, "dp", axis=0, tiled=True)
    width_here = gathered_piece.shape[0]
    shaped_piece = gathered_piece.reshape(width_here, layer_count, channels)
    left_product = jnp.einsum(
        "lrn,nlc->lrc", left_stack, shaped_piece, preferred_element_type=jnp.float32
    )
    preconditioned = jnp.einsum(
        "lrc,lcd->lrd",
        left_product.astype(jnp.bfloat16),
        right_stack,
        preferred_element_type=jnp.float32,
    )
    return (preconditioned, input_grad)


def solution(mesh):
    in_specs = (
        P(None, "dp", "own", None, None),
        P(),
        P("dp", "own", None, None),
        P("dp", "own", None),
        P(),
        P("own", "dp", None),
        P("own", None, None),
    )
    out_specs = (P(None, "dp", None), P("dp", "own", None, None))
    return jax.shard_map(
        per_device, mesh=mesh, in_specs=in_specs, out_specs=out_specs, check_vma=False
    )
```

profile of v0, /device:TPU:0, one launch (start us, length us, event | category | flops | bytes accessed | tf_op | source)
XLA Modules:
  0.0 266.4 jit_solution(8736624988374941266)
XLA Ops:
  9.2 1.3 collective-permute-start.1
  10.5 4.8 %collective-permute-start = (bf16[1,128,128]{1,2,0:T(8,128)(2,1)S(1)}, bf16[1,128,128]{1,2,0:T(8,128)(2,1)S(1)}, u32[]{:S(2)}, u32[]{:S(2)}) collective-permute-start(bf16[1,128,128]{1,2,0:T(8,128)(2,1)S(1)} %get-tuple-element.29), channel_id=1, source_target_pairs={{0,1},{2,3},{4,5},{6,7},{8,9},{10,11},{12,13},{14,15},{16,17},{18,... | collective-permute-start | bytes 98312 | tf_op jit(solution)/shard_map/ppermute | solution.py:16
  15.4 1.3 fusion.111
  21.5 1.6 copy.30
  23.1 1.8 fusion.13
  26.9 5.1 %collective-permute-start.2 = (bf16[1,128,128]{2,1,0:T(8,128)(2,1)}, bf16[1,128,128]{2,1,0:T(8,128)(2,1)S(1)}, u32[]{:S(2)}, u32[]{:S(2)}) collective-permute-start(bf16[1,128,128]{2,1,0:T(8,128)(2,1)} %get-tuple-element.27), channel_id=1, source_target_pairs={{0,1},{2,3},{4,5},{6,7},{8,9},{10,11},{12,13},{14,15},{16,17},{18,... | collective-permute-start | bytes 98312 | tf_op jit(solution)/shard_map/ppermute | solution.py:16
  36.1 2.7 copy.28
  38.8 2.5 copy.20
  41.2 2.7 %fusion.14 = bf16[8,128,128]{2,1,0:T(8,128)(2,1)S(1)} fusion(bf16[8,128,1152]{1,2,0:T(8,128)(2,1)} %bitcast.255, bf16[128,1152,1]{1,0,2:T(8,128)(2,1)} %reshape.135, bf16[4,1,8,128,128]{4,3,2,1,0:T(8,128)(2,1)} %param.7), kind=kOutput, calls=%fused_computation.24 | convolution fusion | flops 302383104 | bytes 3178496 | tf_op jit(solution)/shard_map/dot_general | solution.py:70
  44.6 1.3 collective-permute-start.5
  45.9 5.3 %collective-permute-start.4 = (bf16[1,128,128]{2,1,0:T(8,128)(2,1)}, bf16[1,128,128]{2,1,0:T(8,128)(2,1)S(1)}, u32[]{:S(2)}, u32[]{:S(2)}) collective-permute-start(bf16[1,128,128]{2,1,0:T(8,128)(2,1)} %get-tuple-element.25), channel_id=1, source_target_pairs={{0,1},{2,3},{4,5},{6,7},{8,9},{10,11},{12,13},{14,15},{16,17},{18,... | collective-permute-start | bytes 98312 | tf_op jit(solution)/shard_map/ppermute | solution.py:16
  51.2 1.6 fusion.2
  52.8 1.3 copy.29
  57.2 2.7 copy.26
  59.9 2.5 copy.22
  62.3 2.7 %fusion.15 = bf16[8,128,128]{2,1,0:T(8,128)(2,1)S(1)} fusion(bf16[8,128,1152]{1,2,0:T(8,128)(2,1)} %bitcast.256, bf16[128,1152,1]{1,0,2:T(8,128)(2,1)} %reshape.136, bf16[4,1,8,128,128]{4,3,2,1,0:T(8,128)(2,1)} %param.7), kind=kOutput, calls=%fused_computation.25 | convolution fusion | flops 302383104 | bytes 3178496 | tf_op jit(solution)/shard_map/dot_general | solution.py:70
  67.0 5.1 %collective-permute-start.6 = (bf16[1,128,128]{2,1,0:T(8,128)(2,1)}, bf16[1,128,128]{2,1,0:T(8,128)(2,1)S(1)}, u32[]{:S(2)}, u32[]{:S(2)}) collective-permute-start(bf16[1,128,128]{2,1,0:T(8,128)(2,1)} %get-tuple-element.23), channel_id=1, source_target_pairs={{0,1},{2,3},{4,5},{6,7},{8,9},{10,11},{12,13},{14,15},{16,17},{18,... | collective-permute-start | bytes 98312 | tf_op jit(solution)/shard_map/ppermute | solution.py:16
  72.2 1.6 fusion.1
  73.7 1.3 copy.27
  78.1 2.7 copy.24
  80.8 3.3 %fusion = f32[128,1152]{0,1:T(8,128)} fusion(bf16[1024,128]{1,0:T(8,128)(2,1)S(1)} %bitcast.258, bf16[144,8,8,128]{3,2,1,0:T(8,128)(2,1)} %bitcast.257), kind=kOutput, calls=%fused_computation.4 | convolution fusion | flops 302137344 | bytes 3211264 | tf_op jit(solution)/shard_map/dot_general | solution.py:65
  84.0 2.1 copy.25
  86.2 1.9 mul.59
  88.1 3.0 %pad_maximum_fusion = f32[1152,512]{1,0:T(8,128)} fusion(f32[1152,128]{1,0:T(8,128)S(1)} %mul.68, f32[1152,128]{1,0:T(8,128)} %mul.65, f32[1152,128]{1,0:T(8,128)} %mul.62, f32[1152,128]{1,0:T(8,128)} %mul.59), kind=kLoop, calls=%fused_computation.16 | loop fusion | flops 1769472 | bytes 4718592 | tf_op jit(solution)/shard_map/concatenate | solution.py:80
  103.5 52.2 %reduce-scatter.2.cloned.1.call-done = f32[72,512]{1,0:T(8,128)} async-done(((f32[1152,512]{1,0:T(8,128)}), f32[72,512]{1,0:T(8,128)}) %reduce-scatter.2.cloned.1.call-update) | async-done | bytes 147472 | tf_op jit(solution)/shard_map/reduce_scatter | solution.py:81
  155.7 1.6 convert_element_type.58
  158.1 34.0 %all-reduce.11.cloned.1.call-done = (bf16[72,512]{1,0:T(8,128)(2,1)}, bf16[1,72,1152]{2,1,0:T(8,128)(2,1)}, bf16[1,72,1152]{2,1,0:T(8,128)(2,1)}, bf16[1,72,1152]{2,1,0:T(8,128)(2,1)}, bf16[1,72,1152]{2,1,0:T(8,128)(2,1)}) async-done(((bf16[72,512]{1,0:T(8,128)(2,1)}, bf16[1,72,1152]{2,1,0:T(8,128)(2,1)}, bf16[1,72,1152]{2,1,0:T(8,128)(2,1)}, bf16[1,72,1152]{2,1,0:T(8,128)(2,1)}, ...) | async-done | bytes 737296 | tf_op jit(solution)/shard_map/psum | solution.py:83
  192.4 2.5 copy.32
  194.9 3.3 %fusion.19 = bf16[1,8,128,128]{3,2,1,0:T(8,128)(2,1)} fusion(bf16[8,128,1152]{1,2,0:T(8,128)(2,1)} %bitcast.250, bf16[128,1152,1]{1,0,2:T(8,128)(2,1)S(1)} %reshape.137), kind=kOutput, calls=%fused_computation.30 | convolution fusion | flops 302120960 | bytes 2916352 | tf_op jit(solution)/shard_map/dot_general | solution.py:70
  198.2 18.3 %all-reduce.9.cloned.1.call-done = (bf16[1,128,128]{2,1,0:T(8,128)(2,1)}, bf16[1,128,128]{2,1,0:T(8,128)(2,1)}, bf16[1,128,128]{2,1,0:T(8,128)(2,1)}, bf16[1,128,128]{2,1,0:T(8,128)(2,1)}) async-done(((bf16[1,128,128]{2,1,0:T(8,128)(2,1)}, bf16[1,128,128]{2,1,0:T(8,128)(2,1)}, bf16[1,128,128]{2,1,0:T(8,128)(2,1)}, bf16[1,128,128]{2,1,0:T(8,128)(2,1)}), (bf16[1,128,128]{2,1,0:T(8,128)(2,1)}, ...) | async-done | bytes 131088 | tf_op jit(solution)/shard_map/psum | solution.py:27
  216.5 40.8 %all-gather.2.cloned.1.call-done = bf16[1152,512]{1,0:T(8,128)(2,1)} async-done(((bf16[72,512]{1,0:T(8,128)(2,1)}), bf16[1152,512]{1,0:T(8,128)(2,1)}) %all-gather.2.cloned.1.call-update) | async-done | bytes 1179664 | tf_op jit(solution)/shard_map/all_gather | solution.py:100
  257.3 2.5 fusion.24
  (106 shorter events, 24.5 us)
Async XLA Ops:
  7.2 9.5 %copy-start.3 = (bf16[4,1,8,128,128]{4,3,2,1,0:T(8,128)(2,1)S(1)}, bf16[4,1,8,128,128]{4,3,2,1,0:T(8,128)(2,1)}, u32[]{:S(2)}) copy-start(bf16[4,1,8,128,128]{4,3,2,1,0:T(8,128)(2,1)} %param.7) | copy-start | bytes 3145732
  7.2 148.5 %reduce-scatter.2.cloned.1.call-start = ((), (), s32[]{:S(2)}) async-start(), calls=%async_computation.1 | async-start | bytes 2506752 | tf_op jit(solution)/shard_map/reduce_scatter | solution.py:81
  9.2 11.0 %collective-permute-start.1 = (bf16[1,128,128]{1,2,0:T(8,128)(2,1)S(1)}, bf16[1,128,128]{1,2,0:T(8,128)(2,1)S(1)}, u32[]{:S(2)}, u32[]{:S(2)}) collective-permute-start(bf16[1,128,128]{1,2,0:T(8,128)(2,1)S(1)} %get-tuple-element.30), channel_id=1, source_target_pairs={{1,0},{3,2},{5,4},{7,6},{9,8},{11,10},{13,12},{15,14},{17,16},{19,... | collective-permute-start | bytes 98312 | tf_op jit(solution)/shard_map/ppermute | solution.py:18
  10.5 9.7 %collective-permute-start = (bf16[1,128,128]{1,2,0:T(8,128)(2,1)S(1)}, bf16[1,128,128]{1,2,0:T(8,128)(2,1)S(1)}, u32[]{:S(2)}, u32[]{:S(2)}) collective-permute-start(bf16[1,128,128]{1,2,0:T(8,128)(2,1)S(1)} %get-tuple-element.29), channel_id=1, source_target_pairs={{0,1},{2,3},{4,5},{6,7},{8,9},{10,11},{12,13},{14,15},{16,17},{18,... | collective-permute-start | bytes 98312 | tf_op jit(solution)/shard_map/ppermute | solution.py:16
  23.1 8.9 %copy-start.8 = (bf16[1,1,8,128,128]{4,3,2,1,0:T(8,128)(2,1)S(1)}, bf16[1,1,8,128,128]{4,3,2,1,0:T(8,128)(2,1)}, u32[]{:S(2)}) copy-start(bf16[1,1,8,128,128]{4,3,2,1,0:T(8,128)(2,1)} %get-tuple-element.18) | copy-start | bytes 786436
  25.6 7.5 %collective-permute-start.3 = (bf16[1,128,128]{2,1,0:T(8,128)(2,1)}, bf16[1,128,128]{2,1,0:T(8,128)(2,1)}, u32[]{:S(2)}, u32[]{:S(2)}) collective-permute-start(bf16[1,128,128]{2,1,0:T(8,128)(2,1)} %get-tuple-element.28), channel_id=1, source_target_pairs={{1,0},{3,2},{5,4},{7,6},{9,8},{11,10},{13,12},{15,14},{17,16},{19,... | collective-permute-start | bytes 98312 | tf_op jit(solution)/shard_map/ppermute | solution.py:18
  26.9 7.0 %collective-permute-start.2 = (bf16[1,128,128]{2,1,0:T(8,128)(2,1)}, bf16[1,128,128]{2,1,0:T(8,128)(2,1)S(1)}, u32[]{:S(2)}, u32[]{:S(2)}) collective-permute-start(bf16[1,128,128]{2,1,0:T(8,128)(2,1)} %get-tuple-element.27), channel_id=1, source_target_pairs={{0,1},{2,3},{4,5},{6,7},{8,9},{10,11},{12,13},{14,15},{16,17},{18,... | collective-permute-start | bytes 98312 | tf_op jit(solution)/shard_map/ppermute | solution.py:16
  41.2 10.0 %copy-start = (bf16[8,128,9,128]{1,0,3,2:T(8,128)(2,1)S(1)}, bf16[8,128,9,128]{1,0,3,2:T(8,128)(2,1)}, u32[]{:S(2)}) copy-start(bf16[8,128,9,128]{1,0,3,2:T(8,128)(2,1)} %copy.28) | copy-start | bytes 7077892
  41.2 10.0 %copy-start.7 = (bf16[1,1,8,128,128]{4,3,2,1,0:T(8,128)(2,1)S(1)}, bf16[1,1,8,128,128]{4,3,2,1,0:T(8,128)(2,1)}, u32[]{:S(2)}) copy-start(bf16[1,1,8,128,128]{4,3,2,1,0:T(8,128)(2,1)} %get-tuple-element.16) | copy-start | bytes 786436
  44.6 10.4 %collective-permute-start.5 = (bf16[1,128,128]{2,1,0:T(8,128)(2,1)}, bf16[1,128,128]{2,1,0:T(8,128)(2,1)}, u32[]{:S(2)}, u32[]{:S(2)}) collective-permute-start(bf16[1,128,128]{2,1,0:T(8,128)(2,1)} %get-tuple-element.26), channel_id=1, source_target_pairs={{1,0},{3,2},{5,4},{7,6},{9,8},{11,10},{13,12},{15,14},{17,16},{19,... | collective-permute-start | bytes 98312 | tf_op jit(solution)/shard_map/ppermute | solution.py:18
  45.9 9.1 %collective-permute-start.4 = (bf16[1,128,128]{2,1,0:T(8,128)(2,1)}, bf16[1,128,128]{2,1,0:T(8,128)(2,1)S(1)}, u32[]{:S(2)}, u32[]{:S(2)}) collective-permute-start(bf16[1,128,128]{2,1,0:T(8,128)(2,1)} %get-tuple-element.25), channel_id=1, source_target_pairs={{0,1},{2,3},{4,5},{6,7},{8,9},{10,11},{12,13},{14,15},{16,17},{18,... | collective-permute-start | bytes 98312 | tf_op jit(solution)/shard_map/ppermute | solution.py:16
  62.3 9.8 %copy-start.1 = (bf16[8,128,9,128]{1,0,3,2:T(8,128)(2,1)S(1)}, bf16[8,128,9,128]{1,0,3,2:T(8,128)(2,1)}, u32[]{:S(2)}) copy-start(bf16[8,128,9,128]{1,0,3,2:T(8,128)(2,1)} %copy.26) | copy-start | bytes 7077892
  62.3 9.8 %copy-start.6 = (bf16[1,1,8,128,128]{4,3,2,1,0:T(8,128)(2,1)S(1)}, bf16[1,1,8,128,128]{4,3,2,1,0:T(8,128)(2,1)}, u32[]{:S(2)}) copy-start(bf16[1,1,8,128,128]{4,3,2,1,0:T(8,128)(2,1)} %get-tuple-element.17) | copy-start | bytes 786436
  65.7 10.2 %collective-permute-start.7 = (bf16[1,128,128]{2,1,0:T(8,128)(2,1)}, bf16[1,128,128]{2,1,0:T(8,128)(2,1)}, u32[]{:S(2)}, u32[]{:S(2)}) collective-permute-start(bf16[1,128,128]{2,1,0:T(8,128)(2,1)} %get-tuple-element.24), channel_id=1, source_target_pairs={{1,0},{3,2},{5,4},{7,6},{9,8},{11,10},{13,12},{15,14},{17,16},{19,... | collective-permute-start | bytes 98312 | tf_op jit(solution)/shard_map/ppermute | solution.py:18
  67.0 8.9 %collective-permute-start.6 = (bf16[1,128,128]{2,1,0:T(8,128)(2,1)}, bf16[1,128,128]{2,1,0:T(8,128)(2,1)S(1)}, u32[]{:S(2)}, u32[]{:S(2)}) collective-permute-start(bf16[1,128,128]{2,1,0:T(8,128)(2,1)} %get-tuple-element.23), channel_id=1, source_target_pairs={{0,1},{2,3},{4,5},{6,7},{8,9},{10,11},{12,13},{14,15},{16,17},{18,... | collective-permute-start | bytes 98312 | tf_op jit(solution)/shard_map/ppermute | solution.py:16
  78.1 2.7 %copy-start.5 = (bf16[1,1,8,128,128]{4,3,2,1,0:T(8,128)(2,1)S(1)}, bf16[1,1,8,128,128]{4,3,2,1,0:T(8,128)(2,1)}, u32[]{:S(2)}) copy-start(bf16[1,1,8,128,128]{4,3,2,1,0:T(8,128)(2,1)} %get-tuple-element.15) | copy-start | bytes 786436
  91.1 0.7 copy-start.9
  91.1 11.6 %copy-start.2 = (bf16[2,72,1152]{2,1,0:T(8,128)(2,1)S(1)}, bf16[2,72,1152]{2,1,0:T(8,128)(2,1)}, u32[]{:S(2)}) copy-start(bf16[2,72,1152]{2,1,0:T(8,128)(2,1)} %param.12) | copy-start | bytes 995332
  91.1 66.2 %copy-start.4 = (bf16[2,128,128]{2,1,0:T(8,128)(2,1)S(1)}, bf16[2,128,128]{2,1,0:T(8,128)(2,1)}, u32[]{:S(2)}) copy-start(bf16[2,128,128]{2,1,0:T(8,128)(2,1)} %param.13) | copy-start | bytes 196612
  91.1 100.9 %all-reduce.11.cloned.1.call-start = ((), (), s32[]{:S(2)}) async-start(), calls=%async_computation.4 | async-start | bytes 1474560 | tf_op jit(solution)/shard_map/psum | solution.py:83
  157.3 59.2 %all-reduce.9.cloned.1.call-start = ((), (), s32[]{:S(2)}) async-start(), calls=%async_computation.3 | async-start | bytes 262144 | tf_op jit(solution)/shard_map/psum | solution.py:27
  158.0 99.3 %all-gather.2.cloned.1.call-start = ((), (), s32[]{:S(2)}) async-start(), calls=%async_computation.2 | async-start | bytes 1253376 | tf_op jit(solution)/shard_map/all_gather | solution.py:100
  194.9 62.4 %copy-start.10 = (bf16[1,72,1152]{2,1,0:T(8,128)(2,1)S(1)}, bf16[1,72,1152]{2,1,0:T(8,128)(2,1)}, u32[]{:S(2)}) copy-start(bf16[1,72,1152]{2,1,0:T(8,128)(2,1)} %get-tuple-element.7) | copy-start | bytes 497668
  194.9 62.4 %copy-start.11 = (bf16[1,72,1152]{2,1,0:T(8,128)(2,1)S(1)}, bf16[1,72,1152]{2,1,0:T(8,128)(2,1)}, u32[]{:S(2)}) copy-start(bf16[1,72,1152]{2,1,0:T(8,128)(2,1)} %get-tuple-element.8) | copy-start | bytes 497668
  194.9 62.4 %copy-start.12 = (bf16[1,72,1152]{2,1,0:T(8,128)(2,1)S(1)}, bf16[1,72,1152]{2,1,0:T(8,128)(2,1)}, u32[]{:S(2)}) copy-start(bf16[1,72,1152]{2,1,0:T(8,128)(2,1)} %get-tuple-element.9) | copy-start | bytes 497668
  194.9 62.4 %copy-start.13 = (bf16[1,72,1152]{2,1,0:T(8,128)(2,1)S(1)}, bf16[1,72,1152]{2,1,0:T(8,128)(2,1)}, u32[]{:S(2)}) copy-start(bf16[1,72,1152]{2,1,0:T(8,128)(2,1)} %get-tuple-element.10) | copy-start | bytes 497668
Sparse Core Ops, SparseCore 0:
  91.2 64.3 reduce-scatter.1
  159.0 32.9 all-reduce.10
  194.6 21.8 all-reduce.8
  218.9 38.3 all-gather.1
where the time goes:
time: 268 us; the launch traced here: 266 us
  waiting for transfers between devices  146 us (54%)
  local copies, waits for them, and re-layouts  37.2 us (14%)
  starting transfers between devices  25.7 us (10%)
  between operations  24.6 us (9%)
  matrix products  20.3 us (8%)
  other arithmetic  12.4 us (5%)
    reduce_scatter x1, waiting for transfers between devices, per_device(): lax.psum_scatter(grad_term, 'dp', scatter_dimension=0, tiled=True)  52.2 us
    all_gather x1, waiting for transfers between devices, per_device(): gathered_piece = lax.all_gather(grad_sum, 'dp', axis=0, tiled=True)  40.8 us
    psum x1, waiting for transfers between devices, per_device(): grad_sum = lax.psum(grad_rows.astype(jnp.bfloat16), 'own')  34 us
    ppermute x4, starting transfers between devices, extended(): lax.ppermute(tail, axis, [(i, (i + 1) % count) for i in range(ends)])  20.4 us
    psum x1, waiting for transfers between devices, from_root(): return lax.psum(block, axis)  18.3 us
    another operation x11, local copies, waits for them, and re-layouts, tap_matrix(): stacked = jnp.stack(pieces, axis=2)  17.2 us
    dot_general x4, matrix products, per_device(): lax.dot_general(tap_rows, kernel, (((1,), (1,)), ((), ())), preferred_ele...  10.5 us
    mul x8, local copies, waits for them, and re-layouts, per_device(): grad_block.reshape(9 * channels, channels) * grad_scale  8.66 us
  transfers between devices with their start and end apart: 12, of which 5 were waited for; matrix products, arithmetic and copies ran while one was open for 8% of the time, Pallas kernels for 0%

commit v1 on v0

--- a/solution.py
+++ b/solution.py
@@ -3,6 +3,23 @@
 import jax.numpy as jnp
 from jax import lax
 from jax.sharding import PartitionSpec as P
+
+
+def laid_out(parts, dim):
+    parts = jnp.moveaxis(parts, 0, dim)
+    shape = parts.shape
+    return parts.reshape(*shape[:dim], shape[dim] * shape[dim + 1], *shape[dim + 2 :])
+
+
+def grow_blocks(array, axis):
+    count, index = (lax.axis_size(axis), lax.axis_index(axis))
+    blocks, bit = (array[None], 1)
+    while bit < count:
+        other = lax.ppermute(blocks, axis, [(i, i ^ bit) for i in range(count)])
+        low = index & bit == 0
+        blocks = jnp.concatenate([jnp.where(low, blocks, other), jnp.where(low, other, blocks)])
+        bit *= 2
+    return blocks
 
 
 def extended(cells, sides, width):
@@ -97,7 +114,7 @@
         right_panels.append(right_panel)
     left_stack = jnp.stack(left_panels, axis=0)
     right_stack = jnp.stack(right_panels, axis=0)
-    gathered_piece = lax.all_gather(grad_sum, "dp", axis=0, tiled=True)
+    gathered_piece = laid_out(grow_blocks(grad_sum, "dp"), 0)
     width_here = gathered_piece.shape[0]
     shaped_piece = gathered_piece.reshape(width_here, layer_count, channels)
     left_product = jnp.einsum(

time: 268 us -> 243 us (0.907)
  waiting for transfers between devices: 146 us -> 118 us
  starting transfers between devices: 25.7 us -> 29.4 us
    all_gather x1 -> x0, waiting for transfers between devices: 40.8 us -> none  [per_device(): gathered_piece = lax.all_gather(grad_sum, 'dp', axis=0, tiled=True)]
    ppermute x0 -> x4, waiting for transfers between devices: none -> 30.3 us  [grow_blocks(): other = lax.ppermute(blocks, axis, [(i, i ^ bit) for i in range(count)])]
    psum x1, waiting for transfers between devices: 18.3 us -> 0.02 us  [from_root(): return lax.psum(block, axis)]
    ppermute x0 -> x4, starting transfers between devices: none -> 5.5 us  [grow_blocks(): other = lax.ppermute(blocks, axis, [(i, i ^ bit) for i in range(count)])]
    select_n x0 -> x4, other arithmetic: none -> 3.08 us  [grow_blocks(): jnp.where(low, blocks, other)]
    unnamed x52 -> x56, local copies, waits for them, and re-layouts: 3.66 us -> 5.65 us
  transfers between devices with their start and end apart: 12 -> 15, of which waited for: 5 -> 7; matrix products, arithmetic and copies ran while one was open for 8% -> 8% of each run, Pallas kernels for 0% -> 0%
where the time goes in v1:
time: 243 us; the launch traced here: 242 us
  waiting for transfers between devices  118 us (49%)
  local copies, waits for them, and re-layouts  35.6 us (15%)
  starting transfers between devices  29.4 us (12%)
  between operations  25.2 us (10%)
  matrix products  18.1 us (7%)
  other arithmetic  15 us (6%)
    reduce_scatter x1, waiting for transfers between devices, per_device(): lax.psum_scatter(grad_term, 'dp', scatter_dimension=0, tiled=True)  52.4 us
    psum x1, waiting for transfers between devices, per_device(): grad_sum = lax.psum(grad_rows.astype(jnp.bfloat16), 'own')  34.8 us
    ppermute x4, waiting for transfers between devices, grow_blocks(): other = lax.ppermute(blocks, axis, [(i, i ^ bit) for i in range(count)])  30.3 us
    ppermute x4, starting transfers between devices, extended(): lax.ppermute(tail, axis, [(i, (i + 1) % count) for i in range(ends)])  18.7 us
    another operation x11, local copies, waits for them, and re-layouts, tap_matrix(): stacked = jnp.stack(pieces, axis=2)  17.3 us
    dot_general x4, matrix products, per_device(): lax.dot_general(tap_rows, kernel, (((1,), (1,)), ((), ())), preferred_ele...  10.5 us
    mul x8, local copies, waits for them, and re-layouts, per_device(): grad_block.reshape(9 * channels, channels) * grad_scale  6.53 us
    unnamed x56, local copies, waits for them, and re-layouts  5.65 us
  transfers between devices with their start and end apart: 15, of which 7 were waited for; matrix products, arithmetic and copies ran while one was open for 8% of the time, Pallas kernels for 0%

profile of v1, /device:TPU:0, one launch (start us, length us, event | category | flops | bytes accessed | tf_op | source)
XLA Modules:
  0.0 241.5 jit_solution(6085740306645142518)
XLA Ops:
  10.5 4.8 %collective-permute-start = (bf16[1,128,128]{1,2,0:T(8,128)(2,1)S(1)}, bf16[1,128,128]{1,2,0:T(8,128)(2,1)S(1)}, u32[]{:S(2)}, u32[]{:S(2)}) collective-permute-start(bf16[1,128,128]{1,2,0:T(8,128)(2,1)S(1)} %get-tuple-element.35), channel_id=1, source_target_pairs={{0,1},{2,3},{4,5},{6,7},{8,9},{10,11},{12,13},{14,15},{16,17},{18,... | collective-permute-start | bytes 98312 | tf_op jit(solution)/shard_map/ppermute | solution.py:33
  15.4 1.3 fusion.110
  21.5 1.6 copy.30
  23.1 1.8 fusion.13
  26.3 4.5 %collective-permute-start.2 = (bf16[1,128,128]{2,1,0:T(8,128)(2,1)S(1)}, bf16[1,128,128]{2,1,0:T(8,128)(2,1)S(1)}, u32[]{:S(2)}, u32[]{:S(2)}) collective-permute-start(bf16[1,128,128]{2,1,0:T(8,128)(2,1)S(1)} %get-tuple-element.33), channel_id=1, source_target_pairs={{0,1},{2,3},{4,5},{6,7},{8,9},{10,11},{12,13},{14,15},{16,17},{18,... | collective-permute-start | bytes 98312 | tf_op jit(solution)/shard_map/ppermute | solution.py:33
  34.0 2.7 %copy.28 = bf16[8,128,9,128]{1,0,3,2:T(8,128)(2,1)} copy(bf16[8,128,9,128]{3,1,0,2:T(8,128)(2,1)S(1)} %fusion.81) | data formatting | bytes 4718592 | tf_op jit(solution)/shard_map/stack | solution.py:58
  36.6 2.5 %copy.20 = bf16[8,128,9,128]{1,3,2,0:T(8,128)(2,1)} copy(bf16[8,128,9,128]{3,1,0,2:T(8,128)(2,1)S(1)} %fusion.81) | data formatting | bytes 4718592 | tf_op jit(solution)/shard_map/stack | solution.py:58
  39.1 2.7 %fusion.14 = bf16[8,128,128]{2,1,0:T(8,128)(2,1)S(1)} fusion(bf16[8,128,1152]{1,2,0:T(8,128)(2,1)} %bitcast.245, bf16[128,1152,1]{1,0,2:T(8,128)(2,1)} %reshape.131, bf16[4,1,8,128,128]{4,3,2,1,0:T(8,128)(2,1)} %param.7), kind=kOutput, calls=%fused_computation.24 | convolution fusion | flops 302383104 | bytes 3178496 | tf_op jit(solution)/shard_map/dot_general | solution.py:87
  43.2 4.7 %collective-permute-start.4 = (bf16[1,128,128]{2,1,0:T(8,128)(2,1)S(1)}, bf16[1,128,128]{2,1,0:T(8,128)(2,1)S(1)}, u32[]{:S(2)}, u32[]{:S(2)}) collective-permute-start(bf16[1,128,128]{2,1,0:T(8,128)(2,1)S(1)} %get-tuple-element.31), channel_id=1, source_target_pairs={{0,1},{2,3},{4,5},{6,7},{8,9},{10,11},{12,13},{14,15},{16,17},{18,... | collective-permute-start | bytes 98312 | tf_op jit(solution)/shard_map/ppermute | solution.py:33
  51.9 2.7 %copy.26 = bf16[8,128,9,128]{1,0,3,2:T(8,128)(2,1)} copy(bf16[8,128,9,128]{3,1,0,2:T(8,128)(2,1)S(1)} %fusion.71) | data formatting | bytes 4718592 | tf_op jit(solution)/shard_map/stack | solution.py:58
  54.6 2.5 %copy.22 = bf16[8,128,9,128]{1,3,2,0:T(8,128)(2,1)} copy(bf16[8,128,9,128]{3,1,0,2:T(8,128)(2,1)S(1)} %fusion.71) | data formatting | bytes 4718592 | tf_op jit(solution)/shard_map/stack | solution.py:58
  57.1 2.7 %fusion.15 = bf16[8,128,128]{2,1,0:T(8,128)(2,1)S(1)} fusion(bf16[8,128,1152]{1,2,0:T(8,128)(2,1)} %bitcast.246, bf16[128,1152,1]{1,0,2:T(8,128)(2,1)} %reshape.132, bf16[4,1,8,128,128]{4,3,2,1,0:T(8,128)(2,1)} %param.7), kind=kOutput, calls=%fused_computation.25 | convolution fusion | flops 302383104 | bytes 3178496 | tf_op jit(solution)/shard_map/dot_general | solution.py:87
  61.1 4.5 %collective-permute-start.6 = (bf16[1,128,128]{2,1,0:T(8,128)(2,1)S(1)}, bf16[1,128,128]{2,1,0:T(8,128)(2,1)S(1)}, u32[]{:S(2)}, u32[]{:S(2)}) collective-permute-start(bf16[1,128,128]{2,1,0:T(8,128)(2,1)S(1)} %get-tuple-element.29), channel_id=1, source_target_pairs={{0,1},{2,3},{4,5},{6,7},{8,9},{10,11},{12,13},{14,15},{16,17},{18,... | collective-permute-start | bytes 98312 | tf_op jit(solution)/shard_map/ppermute | solution.py:33
  69.6 2.7 %copy.24 = bf16[8,128,9,128]{1,0,3,2:T(8,128)(2,1)} copy(bf16[8,128,9,128]{3,1,0,2:T(8,128)(2,1)S(1)} %fusion.61) | data formatting | bytes 4718592 | tf_op jit(solution)/shard_map/stack | solution.py:58
  72.3 3.3 %fusion = f32[128,1152]{0,1:T(8,128)} fusion(bf16[1024,128]{1,0:T(8,128)(2,1)S(1)} %bitcast.248, bf16[144,8,8,128]{3,2,1,0:T(8,128)(2,1)} %bitcast.247), kind=kOutput, calls=%fused_computation.4 | convolution fusion | flops 302137344 | bytes 3211264 | tf_op jit(solution)/shard_map/dot_general | solution.py:82
  75.6 2.1 copy.25
  77.7 1.9 mul.59
  79.6 3.0 %pad_maximum_fusion = f32[1152,512]{1,0:T(8,128)} fusion(f32[1152,128]{1,0:T(8,128)S(1)} %mul.68, f32[1152,128]{1,0:T(8,128)} %mul.65, f32[1152,128]{1,0:T(8,128)} %mul.62, f32[1152,128]{1,0:T(8,128)} %mul.59), kind=kLoop, calls=%fused_computation.16 | loop fusion | flops 1769472 | bytes 4718592 | tf_op jit(solution)/shard_map/concatenate | solution.py:97
  95.6 52.4 %reduce-scatter.2.cloned.1.call-done = f32[72,512]{1,0:T(8,128)} async-done(((f32[1152,512]{1,0:T(8,128)}), f32[72,512]{1,0:T(8,128)}) %reduce-scatter.2.cloned.1.call-update) | async-done | bytes 147472 | tf_op jit(solution)/shard_map/reduce_scatter | solution.py:98
  148.0 1.6 convert_bitcast_fusion.2
  149.7 34.8 %all-reduce.11.cloned.1.call-done = (bf16[1,72,512]{2,1,0:T(8,128)(2,1)}, bf16[1,72,1152]{2,1,0:T(8,128)(2,1)}, bf16[1,72,1152]{2,1,0:T(8,128)(2,1)}, bf16[1,72,1152]{2,1,0:T(8,128)(2,1)}, bf16[1,72,1152]{2,1,0:T(8,128)(2,1)}) async-done(((bf16[1,72,512]{2,1,0:T(8,128)(2,1)}, bf16[1,72,1152]{2,1,0:T(8,128)(2,1)}, bf16[1,72,1152]{2,1,0:T(8,128)(2,1)}, bf16[1,72,1152]{2,1,0:T(8,128)(2,1)}, ...) | async-done | bytes 737296 | tf_op jit(solution)/shard_map/psum | solution.py:100
  184.4 1.5 collective-permute-done.8
  186.8 1.5 collective-permute-start.9
  188.4 4.4 %collective-permute-done.9 = bf16[2,72,512]{2,1,0:T(8,128)(2,1)S(1)} collective-permute-done((bf16[2,72,512]{2,1,0:T(8,128)(2,1)S(1)}, bf16[2,72,512]{2,1,0:T(8,128)(2,1)S(1)}, u32[]{:S(2)}, u32[]{:S(2)}) %collective-permute-start.9) | collective-permute-done | bytes 147488 | tf_op jit(solution)/shard_map/ppermute | solution.py:18
  192.9 1.6 collective-permute-start.10
  194.4 6.9 %collective-permute-done.10 = bf16[4,72,512]{2,1,0:T(8,128)(2,1)} collective-permute-done((bf16[4,72,512]{2,1,0:T(8,128)(2,1)S(1)}, bf16[4,72,512]{2,1,0:T(8,128)(2,1)}, u32[]{:S(2)}, u32[]{:S(2)}) %collective-permute-start.10) | collective-permute-done | bytes 294944 | tf_op jit(solution)/shard_map/ppermute | solution.py:18
  203.2 2.4 collective-permute-start.11
  205.6 1.5 dynamic-slice_select_fusion.7
  207.4 2.5 %copy.32 = bf16[8,128,9,128]{1,3,2,0:T(8,128)(2,1)} copy(bf16[8,128,9,128]{3,1,0,2:T(8,128)(2,1)S(1)} %fusion.61) | data formatting | bytes 4718592 | tf_op jit(solution)/shard_map/stack | solution.py:58
  209.9 3.2 %fusion.18 = bf16[1,8,128,128]{3,2,1,0:T(8,128)(2,1)} fusion(bf16[8,128,1152]{1,2,0:T(8,128)(2,1)} %bitcast.240, bf16[128,1152,1]{1,0,2:T(8,128)(2,1)S(1)} %reshape.133), kind=kOutput, calls=%fused_computation.30 | convolution fusion | flops 302120960 | bytes 2916352 | tf_op jit(solution)/shard_map/dot_general | solution.py:87
  213.2 17.5 %collective-permute-done.11 = bf16[8,72,512]{2,1,0:T(8,128)(2,1)} collective-permute-done((bf16[8,72,512]{2,1,0:T(8,128)(2,1)}, bf16[8,72,512]{2,1,0:T(8,128)(2,1)}, u32[]{:S(2)}, u32[]{:S(2)}) %collective-permute-start.11) | collective-permute-done | bytes 589856 | tf_op jit(solution)/shard_map/ppermute | solution.py:18
  233.0 2.0 fusion.23
  (124 shorter events, 30.4 us)
Async XLA Ops:
  7.2 9.5 %copy-start.3 = (bf16[4,1,8,128,128]{4,3,2,1,0:T(8,128)(2,1)S(1)}, bf16[4,1,8,128,128]{4,3,2,1,0:T(8,128)(2,1)}, u32[]{:S(2)}) copy-start(bf16[4,1,8,128,128]{4,3,2,1,0:T(8,128)(2,1)} %param.7) | copy-start | bytes 3145732
  7.2 140.9 %reduce-scatter.2.cloned.1.call-start = ((), (), s32[]{:S(2)}) async-start(), calls=%async_computation.1 | async-start | bytes 2506752 | tf_op jit(solution)/shard_map/reduce_scatter | solution.py:98
  9.2 11.0 %collective-permute-start.1 = (bf16[1,128,128]{1,2,0:T(8,128)(2,1)S(1)}, bf16[1,128,128]{1,2,0:T(8,128)(2,1)S(1)}, u32[]{:S(2)}, u32[]{:S(2)}) collective-permute-start(bf16[1,128,128]{1,2,0:T(8,128)(2,1)S(1)} %get-tuple-element.36), channel_id=1, source_target_pairs={{1,0},{3,2},{5,4},{7,6},{9,8},{11,10},{13,12},{15,14},{17,16},{19,... | collective-permute-start | bytes 98312 | tf_op jit(solution)/shard_map/ppermute | solution.py:35
  10.5 9.7 %collective-permute-start = (bf16[1,128,128]{1,2,0:T(8,128)(2,1)S(1)}, bf16[1,128,128]{1,2,0:T(8,128)(2,1)S(1)}, u32[]{:S(2)}, u32[]{:S(2)}) collective-permute-start(bf16[1,128,128]{1,2,0:T(8,128)(2,1)S(1)} %get-tuple-element.35), channel_id=1, source_target_pairs={{0,1},{2,3},{4,5},{6,7},{8,9},{10,11},{12,13},{14,15},{16,17},{18,... | collective-permute-start | bytes 98312 | tf_op jit(solution)/shard_map/ppermute | solution.py:33
  23.1 7.7 %copy-start.7 = (bf16[1,1,8,128,128]{4,3,2,1,0:T(8,128)(2,1)S(1)}, bf16[1,1,8,128,128]{4,3,2,1,0:T(8,128)(2,1)}, u32[]{:S(2)}) copy-start(bf16[1,1,8,128,128]{4,3,2,1,0:T(8,128)(2,1)} %get-tuple-element.20) | copy-start | bytes 786436
  25.0 6.9 %collective-permute-start.3 = (bf16[1,128,128]{2,1,0:T(8,128)(2,1)S(1)}, bf16[1,128,128]{2,1,0:T(8,128)(2,1)S(1)}, u32[]{:S(2)}, u32[]{:S(2)}) collective-permute-start(bf16[1,128,128]{2,1,0:T(8,128)(2,1)S(1)} %get-tuple-element.34), channel_id=1, source_target_pairs={{1,0},{3,2},{5,4},{7,6},{9,8},{11,10},{13,12},{15,14},{17,16},{19,... | collective-permute-start | bytes 98312 | tf_op jit(solution)/shard_map/ppermute | solution.py:35
  26.3 6.1 %collective-permute-start.2 = (bf16[1,128,128]{2,1,0:T(8,128)(2,1)S(1)}, bf16[1,128,128]{2,1,0:T(8,128)(2,1)S(1)}, u32[]{:S(2)}, u32[]{:S(2)}) collective-permute-start(bf16[1,128,128]{2,1,0:T(8,128)(2,1)S(1)} %get-tuple-element.33), channel_id=1, source_target_pairs={{0,1},{2,3},{4,5},{6,7},{8,9},{10,11},{12,13},{14,15},{16,17},{18,... | collective-permute-start | bytes 98312 | tf_op jit(solution)/shard_map/ppermute | solution.py:33
  31.9 0.6 copy-start.8
  39.1 8.8 %copy-start = (bf16[8,128,9,128]{1,0,3,2:T(8,128)(2,1)S(1)}, bf16[8,128,9,128]{1,0,3,2:T(8,128)(2,1)}, u32[]{:S(2)}) copy-start(bf16[8,128,9,128]{1,0,3,2:T(8,128)(2,1)} %copy.28) | copy-start | bytes 7077892
  39.1 8.8 %copy-start.6 = (bf16[1,1,8,128,128]{4,3,2,1,0:T(8,128)(2,1)S(1)}, bf16[1,1,8,128,128]{4,3,2,1,0:T(8,128)(2,1)}, u32[]{:S(2)}) copy-start(bf16[1,1,8,128,128]{4,3,2,1,0:T(8,128)(2,1)} %get-tuple-element.18) | copy-start | bytes 786436
  41.9 8.0 %collective-permute-start.5 = (bf16[1,128,128]{2,1,0:T(8,128)(2,1)S(1)}, bf16[1,128,128]{2,1,0:T(8,128)(2,1)S(1)}, u32[]{:S(2)}, u32[]{:S(2)}) collective-permute-start(bf16[1,128,128]{2,1,0:T(8,128)(2,1)S(1)} %get-tuple-element.32), channel_id=1, source_target_pairs={{1,0},{3,2},{5,4},{7,6},{9,8},{11,10},{13,12},{15,14},{17,16},{19,... | collective-permute-start | bytes 98312 | tf_op jit(solution)/shard_map/ppermute | solution.py:35
  43.2 6.7 %collective-permute-start.4 = (bf16[1,128,128]{2,1,0:T(8,128)(2,1)S(1)}, bf16[1,128,128]{2,1,0:T(8,128)(2,1)S(1)}, u32[]{:S(2)}, u32[]{:S(2)}) collective-permute-start(bf16[1,128,128]{2,1,0:T(8,128)(2,1)S(1)} %get-tuple-element.31), channel_id=1, source_target_pairs={{0,1},{2,3},{4,5},{6,7},{8,9},{10,11},{12,13},{14,15},{16,17},{18,... | collective-permute-start | bytes 98312 | tf_op jit(solution)/shard_map/ppermute | solution.py:33
  49.8 0.6 copy-start.9
  57.1 8.6 %copy-start.1 = (bf16[8,128,9,128]{1,0,3,2:T(8,128)(2,1)S(1)}, bf16[8,128,9,128]{1,0,3,2:T(8,128)(2,1)}, u32[]{:S(2)}) copy-start(bf16[8,128,9,128]{1,0,3,2:T(8,128)(2,1)} %copy.26) | copy-start | bytes 7077892
  57.1 8.6 %copy-start.5 = (bf16[1,1,8,128,128]{4,3,2,1,0:T(8,128)(2,1)S(1)}, bf16[1,1,8,128,128]{4,3,2,1,0:T(8,128)(2,1)}, u32[]{:S(2)}) copy-start(bf16[1,1,8,128,128]{4,3,2,1,0:T(8,128)(2,1)} %get-tuple-element.19) | copy-start | bytes 786436
  59.8 7.7 %collective-permute-start.7 = (bf16[1,128,128]{2,1,0:T(8,128)(2,1)S(1)}, bf16[1,128,128]{2,1,0:T(8,128)(2,1)S(1)}, u32[]{:S(2)}, u32[]{:S(2)}) collective-permute-start(bf16[1,128,128]{2,1,0:T(8,128)(2,1)S(1)} %get-tuple-element.30), channel_id=1, source_target_pairs={{1,0},{3,2},{5,4},{7,6},{9,8},{11,10},{13,12},{15,14},{17,16},{19,... | collective-permute-start | bytes 98312 | tf_op jit(solution)/shard_map/ppermute | solution.py:35
  61.1 6.5 %collective-permute-start.6 = (bf16[1,128,128]{2,1,0:T(8,128)(2,1)S(1)}, bf16[1,128,128]{2,1,0:T(8,128)(2,1)S(1)}, u32[]{:S(2)}, u32[]{:S(2)}) collective-permute-start(bf16[1,128,128]{2,1,0:T(8,128)(2,1)S(1)} %get-tuple-element.29), channel_id=1, source_target_pairs={{0,1},{2,3},{4,5},{6,7},{8,9},{10,11},{12,13},{14,15},{16,17},{18,... | collective-permute-start | bytes 98312 | tf_op jit(solution)/shard_map/ppermute | solution.py:33
  67.6 0.6 copy-start.10
  69.6 2.7 %copy-start.4 = (bf16[1,1,8,128,128]{4,3,2,1,0:T(8,128)(2,1)S(1)}, bf16[1,1,8,128,128]{4,3,2,1,0:T(8,128)(2,1)}, u32[]{:S(2)}) copy-start(bf16[1,1,8,128,128]{4,3,2,1,0:T(8,128)(2,1)} %get-tuple-element.17) | copy-start | bytes 786436
  82.6 0.7 copy-start.11
  82.6 12.1 %copy-start.2 = (bf16[2,72,1152]{2,1,0:T(8,128)(2,1)S(1)}, bf16[2,72,1152]{2,1,0:T(8,128)(2,1)}, u32[]{:S(2)}) copy-start(bf16[2,72,1152]{2,1,0:T(8,128)(2,1)} %param.12) | copy-start | bytes 995332
  82.6 101.8 %all-reduce.11.cloned.1.call-start = ((), (), s32[]{:S(2)}) async-start(), calls=%async_computation.3 | async-start | bytes 1474560 | tf_op jit(solution)/shard_map/psum | solution.py:100
  149.6 82.7 %all-reduce.9.cloned.1.call-start = ((), (), s32[]{:S(2)}) async-start(), calls=%async_computation.2 | async-start | bytes 262144 | tf_op jit(solution)/shard_map/psum | solution.py:44
  184.4 1.5 collective-permute-start.8
  186.8 6.0 %collective-permute-start.9 = (bf16[2,72,512]{2,1,0:T(8,128)(2,1)S(1)}, bf16[2,72,512]{2,1,0:T(8,128)(2,1)S(1)}, u32[]{:S(2)}, u32[]{:S(2)}) collective-permute-start(bf16[2,72,512]{2,1,0:T(8,128)(2,1)S(1)} %pad_maximum_fusion.12), channel_id=1, source_target_pairs={{0,4},{2,6},{4,0},{6,2},{8,12},{10,14},{12,8},{14,10},{16,20},{18,... | collective-permute-start | bytes 442376 | tf_op jit(solution)/shard_map/ppermute | solution.py:18
  192.9 8.4 %collective-permute-start.10 = (bf16[4,72,512]{2,1,0:T(8,128)(2,1)S(1)}, bf16[4,72,512]{2,1,0:T(8,128)(2,1)}, u32[]{:S(2)}, u32[]{:S(2)}) collective-permute-start(bf16[4,72,512]{2,1,0:T(8,128)(2,1)S(1)} %pad_maximum_fusion.3), channel_id=1, source_target_pairs={{0,8},{2,10},{4,12},{6,14},{8,0},{10,2},{12,4},{14,6},{16,24},{18,... | collective-permute-start | bytes 884744 | tf_op jit(solution)/shard_map/ppermute | solution.py:18
  203.2 27.5 %collective-permute-start.11 = (bf16[8,72,512]{2,1,0:T(8,128)(2,1)}, bf16[8,72,512]{2,1,0:T(8,128)(2,1)}, u32[]{:S(2)}, u32[]{:S(2)}) collective-permute-start(bf16[8,72,512]{2,1,0:T(8,128)(2,1)} %pad_maximum_fusion.2), channel_id=1, source_target_pairs={{0,16},{2,18},{4,20},{6,22},{8,24},{10,26},{12,28},{14,30},{16,0},... | collective-permute-start | bytes 1769480 | tf_op jit(solution)/shard_map/ppermute | solution.py:18
  231.8 0.9 copy-start.12
  231.8 1.0 copy-start.13
  231.8 1.1 copy-start.14
  231.8 1.1 copy-start.15
Sparse Core Ops, SparseCore 0:
  82.8 65.2 reduce-scatter.1
  151.4 32.9 all-reduce.10
  207.2 20.0 all-reduce.8
